TPU v7x, 256 devices: a whole 4x4x8 slice. The times are simulated.
256 devices in a mesh: dp: 32 (over z, y_hi, core), owner: 8 (over y_lo, x).
Axes of the slice: x: 4, y: 4 (y_hi: 2, y_lo: 2; y = y_hi * 2 + y_lo), z: 8, core: 2. Of those that a mesh axis runs over, the one named last changes fastest.
Arguments:
- inputs: bfloat16 [4096, 8192], P('dp'), may hold values from -12 to 12
- out_grads: bfloat16 [4096, 8192], P('dp', 'owner'), may hold values from -16 to 16
- weights: float32 [256, 512, 512], P(('dp', 'owner')), may hold values from -0.0625 to 0.0625
- left_stats: float32 [256, 512, 512], P(('dp', 'owner')), as said below
- right_stats: float32 [256, 512, 512], P(('dp', 'owner')), as said below
- left_roots: float32 [256, 512, 512], P(('dp', 'owner')), as said below
- right_roots: float32 [256, 512, 512], P(('dp', 'owner')), as said below
- refresh: int32 [256], P(('dp', 'owner')), may hold values from 0 to 1, as said below
Outputs:
- new_left_stats: float32 [256, 512, 512], P(('dp', 'owner'))
- new_right_stats: float32 [256, 512, 512], P(('dp', 'owner'))
- new_left_roots: float32 [256, 512, 512], P(('dp', 'owner'))
- new_right_roots: float32 [256, 512, 512], P(('dp', 'owner'))
- update: float32 [256, 512, 512], P(('dp', 'owner'))
- queries: bfloat16 [4096, 8192], P('dp', 'owner')
Inputs may be any that keep to these rules, and one draw needn't show every extreme that they name: For every k, refresh[2k] + refresh[2k + 1] is at most 1, and refresh[0] + refresh[1] is 1. `left_stats`: every block is symmetric positive definite. `right_stats`: every block is symmetric positive definite. `left_roots`: every block is symmetric positive definite. `right_roots`: every block is symmetric positive definite.
All inputs are finite; a program needn't handle non-finite values.
Results may differ from a plain program's by a relative error of at most 0.015.
Values may be sent and summed in bfloat16 or wider, within the bound.
No kernel may reach another device: no remote copies, remote signals or barrier semaphores. Data moves between devices by JAX's collectives and lax.ppermute only.
A program may use at most 128 MiB of HBM per device.

v0:
```python
import math
import jax
import jax.numpy as jnp
from jax import lax
from jax.sharding import PartitionSpec as P

NEWTON = 2
BETA = 0.95
DAMPING = 0.0001


def matmul(left_mat, right_mat):
    return jnp.dot(left_mat, right_mat, preferred_element_type=jnp.float32)


def inverse_root(statistic):
    identity = jnp.eye(statistic.shape[0], dtype=jnp.float32)
    damped = statistic + DAMPING * identity
    factor_z = 2.5 / jnp.sqrt(jnp.sum(damped * damped))
    current = factor_z * damped
    result = jnp.sqrt(jnp.sqrt(factor_z)) * identity
    for turn in range(NEWTON):
        factor = 1.25 * identity - 0.25 * current
        result = matmul(result, factor)
        square = matmul(factor, factor)
        current = matmul(matmul(square, square), current)
    return result


def both_roots(left_stat, right_stat, left_old, right_old):
    return (inverse_root(left_stat), inverse_root(right_stat))


def stale_roots(left_stat, right_stat, left_old, right_old):
    return (left_old, right_old)


def body(inputs, out_grads, weights, left_stats, right_stats, left_roots, right_roots, refresh):
    tok_local, model_width = inputs.shape
    block_size = weights.shape[1]
    col_count = out_grads.shape[1]
    row_blocks = model_width // block_size
    col_blocks = col_count // block_size
    replicas = lax.axis_size("dp")
    tok_total = tok_local * replicas
    x_blocks = inputs.reshape(tok_local, row_blocks, block_size)
    g_blocks = out_grads.reshape(tok_local, col_blocks, block_size)
    feature_send = jnp.repeat(x_blocks, col_blocks, axis=1)
    grad_send = jnp.tile(g_blocks, (1, row_blocks, 1))
    feature_recv, grad_recv = (
        lax.all_to_all(feature_send, "dp", split_axis=1, concat_axis=1, tiled=True),
        lax.all_to_all(grad_send, "dp", split_axis=1, concat_axis=1, tiled=True),
    )
    group_size = 4

    def add_group(turn_index, running):
        x_group = lax.dynamic_slice_in_dim(feature_recv, turn_index * group_size, group_size, 1)
        g_group = lax.dynamic_slice_in_dim(grad_recv, turn_index * group_size, group_size, 1)
        products = (
            jnp.einsum("tsb,tsc->sbc", x_group, g_group, preferred_element_type=jnp.float32)
            / tok_total
        )
        products = lax.optimization_barrier(products.astype(jnp.bfloat16))
        return running + jnp.sum(products.astype(jnp.float32), 0)

    gradient = lax.fori_loop(
        0, replicas // group_size, add_group, jnp.zeros((block_size, block_size), jnp.float32)
    )
    left_new = BETA * left_stats[0] + (1.0 - BETA) * matmul(gradient, gradient.T)
    right_new = BETA * right_stats[0] + (1.0 - BETA) * matmul(gradient.T, gradient)
    refreshing = refresh[0] > 0
    left_root, right_root = lax.cond(
        refreshing, both_roots, stale_roots, left_new, right_new, left_roots[0], right_roots[0]
    )
    direction = matmul(matmul(left_root, gradient), right_root)
    direction = direction * (block_size / jnp.sqrt(jnp.sum(direction * direction) + 1e-12))
    rate = 0.25 / math.sqrt(model_width)
    updated = (weights[0] - rate * direction).astype(jnp.bfloat16)
    partial_out = jnp.einsum(
        "tsb,bc->tsc", feature_recv, updated, preferred_element_type=jnp.float32
    )
    returned = lax.all_to_all(
        partial_out.astype(jnp.bfloat16), "dp", split_axis=1, concat_axis=1, tiled=True
    ).astype(partial_out.dtype)
    queries = returned.reshape(tok_local, row_blocks, col_blocks, block_size).sum(1)
    queries = queries.reshape(tok_local, col_count).astype(jnp.bfloat16)
    return (
        left_new[None],
        right_new[None],
        left_root[None],
        right_root[None],
        direction[None],
        queries,
    )


def solution(mesh):
    in_specs = (
        P("dp", None),
        P("dp", "owner"),
        P(("dp", "owner"), None, None),
        P(("dp", "owner"), None, None),
        P(("dp", "owner"), None, None),
        P(("dp", "owner"), None, None),
        P(("dp", "owner"), None, None),
        P(("dp", "owner")),
    )
    out_specs = (
        P(("dp", "owner"), None, None),
        P(("dp", "owner"), None, None),
        P(("dp", "owner"), None, None),
        P(("dp", "owner"), None, None),
        P(("dp", "owner"), None, None),
        P("dp", "owner"),
    )
    return jax.shard_map(body, mesh=mesh, in_specs=in_specs, out_specs=out_specs, check_vma=False)
```

profile of v0, /device:TPU:4, one launch (start us, length us, event | category | flops | bytes accessed | tf_op | source)
XLA Modules:
  0.0 379.6 jit_solution(8345739376024094570)
XLA Ops:
  0.6 2.4 copy.53
  3.1 0.2 copy.32
  3.3 2.5 broadcast_in_dim.26
  5.8 11.7 %all-to-all-start = ((bf16[128,32,512]{2,0,1:T(8,128)(2,1)}), bf16[128,32,512]{2,0,1:T(8,128)(2,1)}, u32[]{:S(2)}, u32[]{:S(2)}) async-start(bf16[128,32,512]{2,0,1:T(8,128)(2,1)} %bitcast.52), calls=%async_computation | async-start | bytes 8388608 | tf_op jit(solution)/shard_map/all_to_all | solution.py:51
  17.6 96.7 %all-to-all-done = bf16[128,32,512]{2,0,1:T(8,128)(2,1)} async-done(((bf16[128,32,512]{2,0,1:T(8,128)(2,1)}), bf16[128,32,512]{2,0,1:T(8,128)(2,1)}, u32[]{:S(2)}, u32[]{:S(2)}) %all-to-all-start) | async-done | bytes 4194336 | tf_op jit(solution)/shard_map/all_to_all | solution.py:51
  114.2 2.4 tile.11
  116.6 4.9 %all-to-all-start.1 = ((bf16[128,32,512]{2,0,1:T(8,128)(2,1)}), bf16[128,32,512]{2,0,1:T(8,128)(2,1)}, u32[]{:S(2)}, u32[]{:S(2)}) async-start(bf16[128,32,512]{2,0,1:T(8,128)(2,1)} %bitcast.51), calls=%async_computation.1 | async-start | bytes 8388608 | tf_op jit(solution)/shard_map/all_to_all | solution.py:52
  122.2 96.0 %all-to-all-done.1 = bf16[128,32,512]{2,0,1:T(8,128)(2,1)} async-done(((bf16[128,32,512]{2,0,1:T(8,128)(2,1)}), bf16[128,32,512]{2,0,1:T(8,128)(2,1)}, u32[]{:S(2)}, u32[]{:S(2)}) %all-to-all-start.1) | async-done | bytes 4194336 | tf_op jit(solution)/shard_map/all_to_all | solution.py:52
  218.2 21.4 %while.14 = (s32[]{:T(128)}, f32[512,512]{1,0:T(8,128)S(1)}, bf16[128,32,512]{2,0,1:T(8,128)(2,1)}, bf16[128,32,512]{2,0,1:T(8,128)(2,1)}, s32[]{:T(128)}, /*index=5*/s32[]{:T(128)}, s32[]{:T(128)}, s32[]{:T(128)}) while((s32[]{:T(128)}, f32[512,512]{1,0:T(8,128)S(1)}, bf16[128,32,512]{2,0,1:T(8,128)(2,1)}, ...), condition=%wide.region_2.0_spmd.clone, body=%wide.region_0.0_spmd.clone.sunk | while | flops 272891904 | bytes 9438349 | solution.py:66
  218.2 2.0 multiply_convert_fusion.2
  220.2 0.3 convert_reduce_fusion.2
  220.5 0.4 select_add_fusion.14
  220.9 2.0 multiply_convert_fusion.2
  222.9 0.3 convert_reduce_fusion.2
  223.2 0.4 select_add_fusion.14
  223.6 2.0 multiply_convert_fusion.2
  225.5 0.3 convert_reduce_fusion.2
  225.9 0.4 select_add_fusion.14
  226.2 2.0 multiply_convert_fusion.2
  228.2 0.3 convert_reduce_fusion.2
  228.5 0.4 select_add_fusion.14
  228.9 2.0 multiply_convert_fusion.2
  230.9 0.3 convert_reduce_fusion.2
  231.2 0.4 select_add_fusion.14
  231.6 2.0 multiply_convert_fusion.2
  233.6 0.3 convert_reduce_fusion.2
  233.9 0.4 select_add_fusion.14
  234.3 2.0 multiply_convert_fusion.2
  236.2 0.3 convert_reduce_fusion.2
  236.6 0.4 select_add_fusion.14
  236.9 2.0 multiply_convert_fusion.2
  238.9 0.3 convert_reduce_fusion.2
  239.2 0.4 select_add_fusion.14
  239.6 1.8 fusion.98
  241.5 0.5 fusion.99
  242.0 0.4 copy-done.3
  242.5 0.5 copy-done.4
  243.0 2.2 conditional.1
  243.0 1.2 copy.42
  244.2 1.0 copy.43
  245.2 1.0 copy-done.8
  246.1 2.7 multiply_reduce_fusion.2
  249.5 6.9 %convert_bitcast_fusion = bf16[128,32,512]{0,2,1:T(8,128)(2,1)} fusion(bf16[128,32,512]{2,0,1:T(8,128)(2,1)} %all-to-all-done, f32[512,512]{1,0:T(8,128)S(1)} %get-tuple-element.156, f32[1,512,512]{2,1,0:T(8,128)} %param.14, f32[]{:T(128)S(6)} %div.14), kind=kOutput, calls=%fused_computation.69 | convolution fusion | flops 2150629376 | bytes 10485764 | tf_op jit(solution)/shard_map/tsb,bc->tsc/dot_general | solution.py:79
  256.4 22.7 %all-to-all-start.2 = ((bf16[128,32,512]{0,2,1:T(8,128)(2,1)}), bf16[128,32,512]{0,2,1:T(8,128)(2,1)}, u32[]{:S(2)}, u32[]{:S(2)}) async-start(bf16[128,32,512]{0,2,1:T(8,128)(2,1)} %convert_bitcast_fusion), calls=%async_computation.2 | async-start | bytes 8388608 | tf_op jit(solution)/shard_map/all_to_all | solution.py:82
  279.1 1.1 multiply_bitcast_fusion
  280.2 95.6 %all-to-all-done.2 = bf16[128,32,512]{0,2,1:T(8,128)(2,1)} async-done(((bf16[128,32,512]{0,2,1:T(8,128)(2,1)}), bf16[128,32,512]{0,2,1:T(8,128)(2,1)}, u32[]{:S(2)}, u32[]{:S(2)}) %all-to-all-start.2) | async-done | bytes 4194336 | tf_op jit(solution)/shard_map/all_to_all | solution.py:82
  375.8 2.9 reduce
  378.7 0.9 copy.24
  (13 shorter events, 0.1 us)
Async XLA Ops:
  0.6 2.4 copy-start.7
  5.8 11.8 %copy-start.10 = (bf16[128,1024]{1,0:T(8,128)(2,1)S(1)}, bf16[128,1024]{1,0:T(8,128)(2,1)}, u32[]{:S(2)}) copy-start(bf16[128,1024]{1,0:T(8,128)(2,1)} %param.13) | copy-start | bytes 786436
  5.8 108.4 %all-to-all-start = ((bf16[128,32,512]{2,0,1:T(8,128)(2,1)}), bf16[128,32,512]{2,0,1:T(8,128)(2,1)}, u32[]{:S(2)}, u32[]{:S(2)}) async-start(bf16[128,32,512]{2,0,1:T(8,128)(2,1)} %bitcast.52), calls=%async_computation | async-start | bytes 8388608 | tf_op jit(solution)/shard_map/all_to_all | solution.py:51
  116.6 101.6 %all-to-all-start.1 = ((bf16[128,32,512]{2,0,1:T(8,128)(2,1)}), bf16[128,32,512]{2,0,1:T(8,128)(2,1)}, u32[]{:S(2)}, u32[]{:S(2)}) async-start(bf16[128,32,512]{2,0,1:T(8,128)(2,1)} %bitcast.51), calls=%async_computation.1 | async-start | bytes 8388608 | tf_op jit(solution)/shard_map/all_to_all | solution.py:52
  239.6 1.9 copy-start.9
  239.6 2.4 copy-start.2
  241.5 1.0 copy-start.3
  242.0 1.0 copy-start.4
  245.2 1.0 copy-start.8
  256.4 119.4 %all-to-all-start.2 = ((bf16[128,32,512]{0,2,1:T(8,128)(2,1)}), bf16[128,32,512]{0,2,1:T(8,128)(2,1)}, u32[]{:S(2)}, u32[]{:S(2)}) async-start(bf16[128,32,512]{0,2,1:T(8,128)(2,1)} %convert_bitcast_fusion), calls=%async_computation.2 | async-start | bytes 8388608 | tf_op jit(solution)/shard_map/all_to_all | solution.py:82
where the time goes:
time: 380 us
  waiting for transfers between devices  288 us (76%)
  starting transfers between devices  39.3 us (10%)
  matrix products  27.6 us (7%)
  local copies, waits for them, and re-layouts  12.6 us (3%)
  other arithmetic  9.34 us (2%)
    all_to_all x1, waiting for transfers between devices, body(): lax.all_to_all(feature_send, 'dp', split_axis=1, concat_axis=1, tiled=True)  96.7 us
    all_to_all x1, waiting for transfers between devices, body(): lax.all_to_all(grad_send, 'dp', split_axis=1, concat_axis=1, tiled=True)  96 us
    all_to_all x1, waiting for transfers between devices, body(): lax.all_to_all(partial_out.astype(jnp.bfloat16), 'dp', split_axis=1, conc...  95.6 us
    all_to_all x1, starting transfers between devices, body(): lax.all_to_all(partial_out.astype(jnp.bfloat16), 'dp', split_axis=1, conc...  22.7 us
    dot_general x8, matrix products, add_group(): jnp.einsum('tsb,tsc->sbc', x_group, g_group, preferred_element_type=jnp.f...  15.6 us
    all_to_all x1, starting transfers between devices, body(): lax.all_to_all(feature_send, 'dp', split_axis=1, concat_axis=1, tiled=True)  11.7 us
  transfers between devices with their start and end apart: 3, of which 3 were waited for; matrix products, arithmetic and copies ran while one was open for 0% of the time, Pallas kernels for 0%

commit v1 on v0

--- a/solution.py
+++ b/solution.py
@@ -49,7 +49,12 @@
     grad_send = jnp.tile(g_blocks, (1, row_blocks, 1))
     feature_recv, grad_recv = (
         lax.all_to_all(feature_send, "dp", split_axis=1, concat_axis=1, tiled=True),
-        lax.all_to_all(grad_send, "dp", split_axis=1, concat_axis=1, tiled=True),
+        jnp.concatenate(
+            lax.all_to_all(
+                jnp.stack(jnp.split(grad_send, lax.axis_size("dp"), axis=1)), "dp", 0, 0
+            ),
+            axis=1,
+        ),
     )
     group_size = 4
 

time: 380 us -> 398 us (1.047)
  local copies, waits for them, and re-layouts: 12.6 us -> 33.1 us
    unnamed x16 -> x45, local copies, waits for them, and re-layouts: 5.21 us -> 25.5 us
    all_to_all x1, starting transfers between devices: 11.7 us -> 4.89 us  [body(): lax.all_to_all(feature_send, 'dp', split_axis=1, concat_axis=1, tiled=True)]
    all_to_all x1, starting transfers between devices: 4.89 us -> 11.6 us  [body(): lax.all_to_all(jnp.stack(jnp.split(grad_send, lax.axis_size('dp'), axis=1...]
  transfers between devices with their start and end apart: 3 -> 3, of which waited for: 3 -> 3; matrix products, arithmetic and copies ran while one was open for 0% -> 1% of each run, Pallas kernels for 0% -> 0%
where the time goes in v1:
time: 398 us
  waiting for transfers between devices  287 us (72%)
  starting transfers between devices  38.7 us (10%)
  local copies, waits for them, and re-layouts  33.1 us (8%)
  matrix products  27.6 us (7%)
  other arithmetic  9.34 us (2%)
    all_to_all x1, waiting for transfers between devices, body(): lax.all_to_all(feature_send, 'dp', split_axis=1, concat_axis=1, tiled=True)  96 us
    all_to_all x1, waiting for transfers between devices, body(): lax.all_to_all(partial_out.astype(jnp.bfloat16), 'dp', split_axis=1, conc...  95.6 us
    all_to_all x1, waiting for transfers between devices, body(): lax.all_to_all(jnp.stack(jnp.split(grad_send, lax.axis_size('dp'), axis=1...  94.9 us
    unnamed x45, local copies, waits for them, and re-layouts  25.5 us
    all_to_all x1, starting transfers between devices, body(): lax.all_to_all(partial_out.astype(jnp.bfloat16), 'dp', split_axis=1, conc...  22.2 us
    dot_general x8, matrix products, add_group(): jnp.einsum('tsb,tsc->sbc', x_group, g_group, preferred_element_type=jnp.f...  15.6 us
    all_to_all x1, starting transfers between devices, body(): lax.all_to_all(jnp.stack(jnp.split(grad_send, lax.axis_size('dp'), axis=1...  11.6 us
  transfers between devices with their start and end apart: 3, of which 3 were waited for; matrix products, arithmetic and copies ran while one was open for 1% of the time, Pallas kernels for 0%

profile of v1, /device:TPU:4, one launch (start us, length us, event | category | flops | bytes accessed | tf_op | source)
XLA Modules:
  0.0 397.6 jit_solution(16973208922940132974)
XLA Ops:
  0.6 2.3 copy.115
  3.4 0.7 fusion.136
  4.1 0.7 fusion.135
  4.8 0.7 fusion.134
  5.4 0.7 fusion.133
  6.7 0.7 fusion.131
  7.4 0.7 fusion.130
  8.1 0.7 fusion.129
  8.7 0.7 fusion.128
  10.0 0.7 fusion.126
  11.4 0.7 fusion.124
  12.7 0.7 fusion.122
  13.3 0.7 fusion.121
  15.3 0.7 fusion.118
  16.6 0.7 fusion.116
  17.9 0.7 fusion.114
  18.6 0.7 fusion.113
  19.2 0.7 fusion.112
  19.9 0.7 fusion.111
  21.9 0.7 fusion.108
  23.2 0.7 fusion.106
  24.5 11.6 %all-to-all-start.1 = ((bf16[32,128,1,512]{3,1,2,0:T(8,128)(2,1)}), bf16[32,128,1,512]{3,1,2,0:T(8,128)(2,1)}, u32[]{:S(2)}, u32[]{:S(2)}) async-start(bf16[32,128,1,512]{3,1,2,0:T(8,128)(2,1)} %fusion.105), calls=%async_computation.1 | async-start | bytes 8388608 | tf_op jit(solution)/shard_map/all_to_all | solution.py:53
  36.1 1.8 copy.63
  37.9 94.9 %all-to-all-done.1 = bf16[32,128,1,512]{3,1,2,0:T(8,128)(2,1)} async-done(((bf16[32,128,1,512]{3,1,2,0:T(8,128)(2,1)}), bf16[32,128,1,512]{3,1,2,0:T(8,128)(2,1)}, u32[]{:S(2)}, u32[]{:S(2)}) %all-to-all-start.1) | async-done | bytes 4194336 | tf_op jit(solution)/shard_map/all_to_all | solution.py:53
  132.8 2.4 broadcast_in_dim.26
  135.2 4.9 %all-to-all-start = ((bf16[128,32,512]{2,0,1:T(8,128)(2,1)}), bf16[128,32,512]{2,0,1:T(8,128)(2,1)}, u32[]{:S(2)}, u32[]{:S(2)}) async-start(bf16[128,32,512]{2,0,1:T(8,128)(2,1)} %bitcast.214), calls=%async_computation | async-start | bytes 8388608 | tf_op jit(solution)/shard_map/all_to_all | solution.py:51
  140.8 96.0 %all-to-all-done = bf16[128,32,512]{2,0,1:T(8,128)(2,1)} async-done(((bf16[128,32,512]{2,0,1:T(8,128)(2,1)}), bf16[128,32,512]{2,0,1:T(8,128)(2,1)}, u32[]{:S(2)}, u32[]{:S(2)}) %all-to-all-start) | async-done | bytes 4194336 | tf_op jit(solution)/shard_map/all_to_all | solution.py:51
  236.8 21.4 %while.14 = (s32[]{:T(128)}, f32[512,512]{1,0:T(8,128)S(1)}, bf16[128,32,512]{2,0,1:T(8,128)(2,1)}, bf16[128,32,512]{2,0,1:T(8,128)(2,1)}, s32[]{:T(128)}, /*index=5*/s32[]{:T(128)}, s32[]{:T(128)}, s32[]{:T(128)}) while((s32[]{:T(128)}, f32[512,512]{1,0:T(8,128)S(1)}, bf16[128,32,512]{2,0,1:T(8,128)(2,1)}, ...), condition=%wide.region_2.0_spmd.clone, body=%wide.region_0.0_spmd.clone.sunk | while | flops 272891904 | bytes 9438349 | solution.py:71
  236.8 2.0 multiply_convert_fusion.2
  239.5 2.0 multiply_convert_fusion.2
  242.2 2.0 multiply_convert_fusion.2
  244.8 2.0 multiply_convert_fusion.2
  247.5 2.0 multiply_convert_fusion.2
  250.2 2.0 multiply_convert_fusion.2
  252.9 2.0 multiply_convert_fusion.2
  255.5 2.0 multiply_convert_fusion.2
  258.2 1.8 fusion.98
  261.6 2.2 conditional.1
  261.6 1.2 copy.104
  262.8 1.0 copy.105
  263.8 1.0 copy-done.7
  264.7 2.7 multiply_reduce_fusion.2
  268.1 6.9 %convert_bitcast_fusion = bf16[128,32,512]{0,2,1:T(8,128)(2,1)} fusion(bf16[128,32,512]{2,0,1:T(8,128)(2,1)} %all-to-all-done, f32[512,512]{1,0:T(8,128)S(1)} %get-tuple-element.156, f32[1,512,512]{2,1,0:T(8,128)} %param.14, f32[]{:T(128)S(6)} %div.14), kind=kOutput, calls=%fused_computation.69 | convolution fusion | flops 2150629376 | bytes 10485764 | tf_op jit(solution)/shard_map/tsb,bc->tsc/dot_general | solution.py:84
  275.0 22.2 %all-to-all-start.2 = ((bf16[128,32,512]{0,2,1:T(8,128)(2,1)}), bf16[128,32,512]{0,2,1:T(8,128)(2,1)}, u32[]{:S(2)}, u32[]{:S(2)}) async-start(bf16[128,32,512]{0,2,1:T(8,128)(2,1)} %convert_bitcast_fusion), calls=%async_computation.2 | async-start | bytes 8388608 | tf_op jit(solution)/shard_map/all_to_all | solution.py:87
  297.2 1.1 multiply_bitcast_fusion
  298.3 95.6 %all-to-all-done.2 = bf16[128,32,512]{0,2,1:T(8,128)(2,1)} async-done(((bf16[128,32,512]{0,2,1:T(8,128)(2,1)}), bf16[128,32,512]{0,2,1:T(8,128)(2,1)}, u32[]{:S(2)}, u32[]{:S(2)}) %all-to-all-start.2) | async-done | bytes 4194336 | tf_op jit(solution)/shard_map/all_to_all | solution.py:87
  393.9 2.9 reduce
  396.8 0.9 copy.55
  (43 shorter events, 15.1 us)
Async XLA Ops:
  0.6 2.3 copy-start.9
  24.5 108.3 %all-to-all-start.1 = ((bf16[32,128,1,512]{3,1,2,0:T(8,128)(2,1)}), bf16[32,128,1,512]{3,1,2,0:T(8,128)(2,1)}, u32[]{:S(2)}, u32[]{:S(2)}) async-start(bf16[32,128,1,512]{3,1,2,0:T(8,128)(2,1)} %fusion.105), calls=%async_computation.1 | async-start | bytes 8388608 | tf_op jit(solution)/shard_map/all_to_all | solution.py:53
  135.2 101.6 %all-to-all-start = ((bf16[128,32,512]{2,0,1:T(8,128)(2,1)}), bf16[128,32,512]{2,0,1:T(8,128)(2,1)}, u32[]{:S(2)}, u32[]{:S(2)}) async-start(bf16[128,32,512]{2,0,1:T(8,128)(2,1)} %bitcast.214), calls=%async_computation | async-start | bytes 8388608 | tf_op jit(solution)/shard_map/all_to_all | solution.py:51
  258.2 1.9 copy-start.8
  258.2 2.4 copy-start.2
  260.1 1.0 copy-start.3
  260.6 1.0 copy-start.4
  263.8 1.0 copy-start.7
  275.0 118.9 %all-to-all-start.2 = ((bf16[128,32,512]{0,2,1:T(8,128)(2,1)}), bf16[128,32,512]{0,2,1:T(8,128)(2,1)}, u32[]{:S(2)}, u32[]{:S(2)}) async-start(bf16[128,32,512]{0,2,1:T(8,128)(2,1)} %convert_bitcast_fusion), calls=%async_computation.2 | async-start | bytes 8388608 | tf_op jit(solution)/shard_map/all_to_all | solution.py:87
